TPU v7x, 512 devices: a whole 4x4x16 slice. The times are simulated.
512 devices in a mesh: section: 8 (over y, x_hi), ctx: 16 (over z), dp: 4 (over x_lo, core).
Axes of the slice: x: 4 (x_hi: 2, x_lo: 2; x = x_hi * 2 + x_lo), y: 4, z: 16, core: 2. Of those that a mesh axis runs over, the one named last changes fastest.
Arguments:
- activations: bfloat16 [8, 4, 2048, 1280], P('section', 'dp', 'ctx'), may hold values from -6 to 6
- out_grads: bfloat16 [8, 4, 2048, 1280], P('section', 'dp', 'ctx'), may hold values from -6 to 6
- doc_ids: int32 [4, 16], replicated, may hold values from 0 to 3, never falling along the last dimension, each value on 1 to 12 neighbouring positions
- query_weight: bfloat16 [8, 1280, 640], P('section', None, 'dp'), may hold values from -0.195655948 to 0.195655948
- key_weight: bfloat16 [8, 1280, 640], P('section', None, 'dp'), may hold values from -3.0745935 to 3.0745935
- value_weight: bfloat16 [8, 1280, 640], P('section', None, 'dp'), may hold values from -0.15625 to 0.15625
- out_weight: bfloat16 [8, 640, 1280], P('section', 'dp'), may hold values from -0.25 to 0.25
Outputs:
- received_grad: bfloat16 [8, 4, 2048, 1280], P('section', 'dp', 'ctx')
Inputs may be any that keep to these rules, and one draw needn't show every extreme that they name: `doc_ids`: each page stack's documents are runs of whole blocks, numbered from 0 in order; a document covers at most 12 blocks.
All inputs are finite; a program needn't handle non-finite values.
Results may differ from a plain program's by a relative error of at most 0.0085.
The roundings to bfloat16 on the way count: a program that leaves them out, or rounds other values in their place, can miss the bound.
Values may be sent and summed in bfloat16 or wider, within the bound.
A program may use at most 128 MiB of HBM per device.

v0:
```python
import math
import jax
import jax.numpy as jnp
from jax import lax
from jax.sharding import PartitionSpec as P

HEAD_DIM = 80
BLOCK = 128
NEG = -1e30
HIGHEST = lax.Precision.HIGHEST


def from_behind(array, axis, by):
    length = lax.axis_size(axis)
    return lax.ppermute(array, axis, [(i, (i + by) % length) for i in range(length)])


def expand(allowed_blocks, query_len, key_len):
    page_count = allowed_blocks.shape[0]
    query_blocks = query_len // BLOCK
    key_blocks = key_len // BLOCK
    widened = jnp.broadcast_to(
        allowed_blocks[:, :, None, :, None], (page_count, query_blocks, BLOCK, key_blocks, BLOCK)
    )
    return widened.reshape(page_count, query_len, key_len)


def row_statistics(
    queries, out_grad, all_keys, all_values, block_table, my_offset, head_count, score_scale
):
    page_count, row_count, _ = queries.shape
    length = all_keys.shape[1]
    block_len = math.gcd(length, 512)
    query_four = queries.reshape(page_count, row_count, head_count, HEAD_DIM)
    grad_four = out_grad.reshape(page_count, row_count, head_count, HEAD_DIM)
    my_blocks = lax.dynamic_slice_in_dim(block_table, my_offset // BLOCK, row_count // BLOCK, 1)

    def row_visit(index, totals):
        key_offset = index * block_len
        key_block = lax.dynamic_slice_in_dim(all_keys, key_offset, block_len, 1).reshape(
            page_count, block_len, head_count, HEAD_DIM
        )
        value_block = lax.dynamic_slice_in_dim(all_values, key_offset, block_len, 1).reshape(
            page_count, block_len, head_count, HEAD_DIM
        )
        allowed = expand(
            lax.dynamic_slice_in_dim(my_blocks, key_offset // BLOCK, block_len // BLOCK, 2),
            row_count,
            block_len,
        )[:, None]
        old_max, old_sum, old_dot = totals
        scores = (
            jnp.einsum(
                "brhd,bkhd->bhrk",
                query_four,
                key_block,
                precision=HIGHEST,
                preferred_element_type=jnp.float32,
            )
            * score_scale
        )
        scores = jnp.where(allowed, scores, NEG)
        new_max = jnp.maximum(old_max, jnp.max(scores, axis=-1))
        weights = jnp.where(allowed, jnp.exp(scores - new_max[..., None]), 0.0)
        dprob = jnp.einsum(
            "brhd,bkhd->bhrk", grad_four, value_block, preferred_element_type=jnp.float32
        )
        factor = jnp.exp(old_max - new_max)
        return (
            new_max,
            old_sum * factor + jnp.sum(weights, axis=-1),
            old_dot * factor + jnp.sum(weights * dprob, axis=-1),
        )

    stat_shape = (page_count, head_count, row_count)
    zeros = jnp.zeros(stat_shape, jnp.float32)
    start_state = (jnp.full(stat_shape, NEG, jnp.float32), zeros, zeros)
    final_max, final_sum, final_dot = lax.fori_loop(0, length // block_len, row_visit, start_state)
    log_total = final_max + jnp.log(final_sum)
    row_delta = final_dot / final_sum
    return (jnp.transpose(log_total, (0, 2, 1)), jnp.transpose(row_delta, (0, 2, 1)))


def query_side(
    queries,
    out_grad,
    all_keys,
    all_values,
    block_table,
    my_offset,
    log_total,
    row_delta,
    head_count,
    score_scale,
):
    page_count, row_count, width = queries.shape
    length = all_keys.shape[1]
    block_len = math.gcd(length, 512)
    query_four = queries.reshape(page_count, row_count, head_count, HEAD_DIM)
    grad_four = out_grad.reshape(page_count, row_count, head_count, HEAD_DIM)
    log_heads = jnp.transpose(log_total, (0, 2, 1))
    delta_heads = jnp.transpose(row_delta, (0, 2, 1))
    my_blocks = lax.dynamic_slice_in_dim(block_table, my_offset // BLOCK, row_count // BLOCK, 1)

    def query_visit(index, totals):
        key_offset = index * block_len
        key_block = lax.dynamic_slice_in_dim(all_keys, key_offset, block_len, 1).reshape(
            page_count, block_len, head_count, HEAD_DIM
        )
        value_block = lax.dynamic_slice_in_dim(all_values, key_offset, block_len, 1).reshape(
            page_count, block_len, head_count, HEAD_DIM
        )
        allowed = expand(
            lax.dynamic_slice_in_dim(my_blocks, key_offset // BLOCK, block_len // BLOCK, 2),
            row_count,
            block_len,
        )[:, None]
        scores = (
            jnp.einsum(
                "brhd,bkhd->bhrk",
                query_four,
                key_block,
                precision=HIGHEST,
                preferred_element_type=jnp.float32,
            )
            * score_scale
        )
        scores = jnp.where(allowed, scores, NEG)
        prob = jnp.where(allowed, jnp.exp(scores - log_heads[..., None]), 0.0)
        dprob = jnp.einsum(
            "brhd,bkhd->bhrk", grad_four, value_block, preferred_element_type=jnp.float32
        )
        dscore = prob * (dprob - delta_heads[..., None])
        dscore_low = dscore.astype(jnp.bfloat16).astype(jnp.float32)
        return totals + jnp.einsum(
            "bhrk,bkhd->brhd",
            dscore_low,
            key_block,
            precision=HIGHEST,
            preferred_element_type=jnp.float32,
        )

    start_state = jnp.zeros((page_count, row_count, head_count, HEAD_DIM), jnp.float32)
    summed = lax.fori_loop(0, length // block_len, query_visit, start_state)
    return (summed * score_scale).astype(jnp.bfloat16).reshape(page_count, row_count, width)


def key_side(
    totals,
    portion,
    key_rows,
    value_rows,
    all_log_total,
    all_delta,
    block_table,
    my_offset,
    head_count,
    score_scale,
):
    part_queries, part_grads = portion
    page_count, part_len, _ = part_queries.shape
    row_count = key_rows.shape[1]
    block_len = math.gcd(part_len, 512)
    key_four = key_rows.reshape(page_count, row_count, head_count, HEAD_DIM)
    value_four = value_rows.reshape(page_count, row_count, head_count, HEAD_DIM)
    key_columns = lax.dynamic_slice_in_dim(block_table, my_offset // BLOCK, row_count // BLOCK, 2)

    def key_visit(index, state):
        query_offset = index * block_len
        query_part = lax.dynamic_slice_in_dim(part_queries, query_offset, block_len, 1).reshape(
            page_count, block_len, head_count, HEAD_DIM
        )
        grad_part = (
            lax.dynamic_slice_in_dim(part_grads, query_offset, block_len, 1)
            .astype(jnp.bfloat16)
            .reshape(page_count, block_len, head_count, HEAD_DIM)
        )
        log_part = jnp.transpose(
            lax.dynamic_slice_in_dim(all_log_total, query_offset, block_len, 1), (0, 2, 1)
        )
        delta_part = jnp.transpose(
            lax.dynamic_slice_in_dim(all_delta, query_offset, block_len, 1), (0, 2, 1)
        )
        allowed = expand(
            lax.dynamic_slice_in_dim(key_columns, query_offset // BLOCK, block_len // BLOCK, 1),
            block_len,
            row_count,
        )[:, None]
        key_total, value_total = state
        scores = (
            jnp.einsum(
                "bphd,brhd->bhpr",
                query_part,
                key_four,
                precision=HIGHEST,
                preferred_element_type=jnp.float32,
            )
            * score_scale
        )
        scores = jnp.where(allowed, scores, NEG)
        prob = jnp.where(allowed, jnp.exp(scores - log_part[..., None]), 0.0)
        value_total = value_total + jnp.einsum(
            "bhpr,bphd->brhd",
            prob.astype(jnp.bfloat16),
            grad_part,
            preferred_element_type=jnp.float32,
        )
        dprob = jnp.einsum(
            "bphd,brhd->bhpr", grad_part, value_four, preferred_element_type=jnp.float32
        )
        dscore = prob * (dprob - delta_part[..., None])
        dscore_low = dscore.astype(jnp.bfloat16).astype(jnp.float32)
        key_total = key_total + jnp.einsum(
            "bhpr,bphd->brhd",
            dscore_low,
            query_part,
            precision=HIGHEST,
            preferred_element_type=jnp.float32,
        )
        return (key_total, value_total)

    return lax.fori_loop(0, part_len // block_len, key_visit, totals)


def body(activations, out_grads, doc_ids, query_weight, key_weight, value_weight, out_weight):
    score_scale = HEAD_DIM ** (-0.5)
    row_count = activations.shape[2]
    my_offset = lax.axis_index("ctx") * row_count
    full_query, full_key, full_value, full_out = (
        lax.all_gather(query_weight, "dp", axis=2, tiled=True),
        lax.all_gather(key_weight, "dp", axis=2, tiled=True),
        lax.all_gather(value_weight, "dp", axis=2, tiled=True),
        lax.all_gather(out_weight, "dp", axis=1, tiled=True),
    )
    page_inputs = activations[0]
    page_upstream = out_grads[0]
    page_ids = lax.dynamic_slice_in_dim(doc_ids, lax.axis_index("dp"), 1, 0)
    proj_query = full_query[0]
    proj_key = full_key[0]
    proj_value = full_value[0]
    proj_out = full_out[0]
    head_count = proj_query.shape[1] // HEAD_DIM
    inputs = page_inputs.astype(jnp.float32)
    inv_rms = lax.rsqrt(jnp.mean(inputs * inputs, axis=-1, keepdims=True) + 1e-05)
    normed = (inputs * inv_rms).astype(jnp.bfloat16)
    queries = jnp.einsum("brd,dh->brh", normed, proj_query, preferred_element_type=jnp.float32)
    key_rows = jnp.einsum("brd,dh->brh", normed, proj_key, preferred_element_type=jnp.float32)
    value_rows = jnp.einsum(
        "brd,dh->brh", normed, proj_value, preferred_element_type=jnp.float32
    ).astype(jnp.bfloat16)
    out_grad = jnp.einsum(
        "brd,hd->brh", page_upstream, proj_out, preferred_element_type=jnp.float32
    ).astype(jnp.bfloat16)
    block_table = page_ids[:, :, None] == page_ids[:, None, :]
    all_keys, wide_values = (
        lax.all_gather(key_rows, "ctx", axis=1, tiled=True),
        lax.all_gather(value_rows.astype(jnp.float32), "ctx", axis=1, tiled=True),
    )
    all_values = wide_values.astype(jnp.bfloat16)
    log_total, row_delta = row_statistics(
        queries, out_grad, all_keys, all_values, block_table, my_offset, head_count, score_scale
    )
    all_log_total, all_delta = (
        lax.all_gather(log_total, "ctx", axis=1, tiled=True),
        lax.all_gather(row_delta, "ctx", axis=1, tiled=True),
    )
    q_grad = query_side(
        queries,
        out_grad,
        all_keys,
        all_values,
        block_table,
        my_offset,
        log_total,
        row_delta,
        head_count,
        score_scale,
    )
    empty = jnp.zeros((key_rows.shape[0], row_count, head_count, HEAD_DIM), jnp.float32)
    key_total, value_total = key_side(
        (empty, empty),
        (
            lax.all_gather(queries, "ctx", axis=1, tiled=True),
            lax.all_gather(out_grad.astype(jnp.float32), "ctx", axis=1, tiled=True),
        ),
        key_rows,
        value_rows,
        all_log_total,
        all_delta,
        block_table,
        my_offset,
        head_count,
        score_scale,
    )
    k_grad = (key_total * score_scale).astype(jnp.bfloat16).reshape(key_rows.shape)
    v_grad = value_total.astype(jnp.bfloat16).reshape(value_rows.shape)
    summed = jnp.einsum("brh,dh->brd", q_grad, proj_query, preferred_element_type=jnp.float32)
    summed = summed + jnp.einsum(
        "brh,dh->brd", k_grad, proj_key, preferred_element_type=jnp.float32
    )
    normed_grad = summed + jnp.einsum(
        "brh,dh->brd", v_grad, proj_value, preferred_element_type=jnp.float32
    )
    branch = inv_rms * normed_grad - inputs * inv_rms**3 * jnp.mean(
        normed_grad * inputs, axis=-1, keepdims=True
    )
    branch_grad = branch.astype(jnp.bfloat16)[None]
    return from_behind(branch_grad, "section", -1)


def solution(mesh):
    return jax.shard_map(
        body,
        mesh=mesh,
        in_specs=(
            P("section", "dp", "ctx", None),
            P("section", "dp", "ctx", None),
            P(),
            P("section", None, "dp"),
            P("section", None, "dp"),
            P("section", None, "dp"),
            P("section", "dp", None),
        ),
        out_specs=P("section", "dp", "ctx", None),
        check_vma=False,
    )
```

profile of v0, /device:TPU:62, one launch (start us, length us, event | category | flops | bytes accessed | tf_op | source)
XLA Modules:
  0.0 580.7 jit_solution(2038924234252000097)
XLA Ops:
  10.5 35.1 %all-gather.17.cloned.1.call-done = bf16[1,1280,640]{1,2,0:T(8,128)(2,1)} async-done(((bf16[1,1280,160]{1,2,0:T(8,128)(2,1)}), bf16[1,1280,640]{1,2,0:T(8,128)(2,1)}) %all-gather.17.cloned.1.call-update) | async-done | bytes 1638416 | tf_op jit(solution)/shard_map/all_gather | solution.py:232
  45.6 2.7 fusion.28
  48.4 33.3 %all-gather.13.cloned.1.call-done = bf16[1,1280,640]{1,2,0:T(8,128)(2,1)} async-done(((bf16[1,1280,160]{1,2,0:T(8,128)(2,1)}), bf16[1,1280,640]{1,2,0:T(8,128)(2,1)}) %all-gather.13.cloned.1.call-update) | async-done | bytes 1638416 | tf_op jit(solution)/shard_map/all_gather | solution.py:231
  81.7 2.8 fusion.26
  84.6 33.3 %all-gather.19.cloned.1.call-done = bf16[1,640,1280]{2,1,0:T(8,128)(2,1)} async-done(((bf16[1,160,1280]{2,1,0:T(8,128)(2,1)}), bf16[1,640,1280]{2,1,0:T(8,128)(2,1)}) %all-gather.19.cloned.1.call-update) | async-done | bytes 1638416 | tf_op jit(solution)/shard_map/all_gather | solution.py:233
  117.8 2.7 fusion.31
  124.9 28.9 %all-gather.15.cloned.1.call-done = bf16[1,1280,640]{1,2,0:T(8,128)(2,1)} async-done(((bf16[1,1280,160]{1,2,0:T(8,128)(2,1)}), bf16[1,1280,640]{1,2,0:T(8,128)(2,1)}) %all-gather.15.cloned.1.call-update) | async-done | bytes 1638416 | tf_op jit(solution)/shard_map/all_gather | solution.py:230
  153.8 2.1 fusion.23
  158.1 74.2 %all-gather.23.cloned.1.call-done = bf16[2048,640]{1,0:T(8,128)(2,1)} async-done(((bf16[128,640]{1,0:T(8,128)(2,1)}), bf16[2048,640]{1,0:T(8,128)(2,1)}) %all-gather.23.cloned.1.call-update) | async-done | bytes 2621456 | tf_op jit(solution)/shard_map/all_gather | solution.py:257
  232.4 4.5 copy.22
  236.8 74.7 %all-gather.21.cloned.1.call-done = f32[2048,640]{1,0:T(8,128)} async-done(((f32[128,640]{1,0:T(8,128)}), f32[2048,640]{1,0:T(8,128)}) %all-gather.21.cloned.1.call-update) | async-done | bytes 5242896 | tf_op jit(solution)/shard_map/all_gather | solution.py:256
  311.6 6.0 %copy.23 = f32[1,2048,640]{1,2,0:T(8,128)} copy(f32[1,2048,640]{2,1,0:T(8,128)} %bitcast.272) | data formatting | bytes 10485760
  317.6 42.2 %while.54 = (s32[]{:T(128)}, f32[1,8,128]{2,1,0:T(8,128)S(1)}, f32[1,8,128]{2,1,0:T(8,128)S(1)}, f32[1,8,128]{2,1,0:T(8,128)S(1)}, pred[1,1,16]{2,1,0:T(4,128)(4...) while((s32[]{:T(128)}, f32[1,8,128]{2,1,0:T(8,128)S(1)}, ...), condition=%wide.region_5.6_spmd.clone, body=%wide.region_1.5_spmd.clone.sunk | while | flops 594549760 | bytes 12757413 | solution.py:78
  317.6 2.0 constant_dynamic-slice_fusion.16
  321.8 3.6 bitcast_reduce_fusion.2
  325.4 2.0 fusion.91
  328.1 2.0 constant_dynamic-slice_fusion.16
  332.3 3.6 bitcast_reduce_fusion.2
  336.0 2.1 fusion.91
  338.7 2.0 constant_dynamic-slice_fusion.16
  342.9 3.6 bitcast_reduce_fusion.2
  346.5 2.0 fusion.91
  349.2 2.0 constant_dynamic-slice_fusion.16
  353.4 3.6 bitcast_reduce_fusion.2
  357.1 2.0 fusion.91
  359.8 29.6 %all_gather.37 = f32[1,2048,8]{1,2,0:T(8,128)} all-gather(f32[1,128,8]{1,2,0:T(8,128)S(1)} %bitcast.287), channel_id=1, replica_groups=mesh['section'=8,'ctx'=16,'dp'=4] {'ctx'}, dimensions={1}, use_global_device_ids=true | all-gather | bytes 69632 | tf_op jit(solution)/shard_map/all_gather | solution.py:264
  389.4 30.9 %all_gather.39 = f32[1,2048,8]{1,2,0:T(8,128)} all-gather(f32[1,128,8]{1,2,0:T(8,128)S(1)} %bitcast.285), channel_id=1, replica_groups=mesh['section'=8,'ctx'=16,'dp'=4] {'ctx'}, dimensions={1}, use_global_device_ids=true | all-gather | bytes 69632 | tf_op jit(solution)/shard_map/all_gather | solution.py:265
  420.3 56.8 %while.55 = (s32[]{:T(128)}, f32[1,128,8,80]{1,3,2,0:T(8,128)}, f32[1,2048,640]{1,2,0:T(8,128)}, pred[1,1,16]{2,1,0:T(4,128)(4,1)}, f32[1,128,8,80]{3,2,1,0:T(8,...) while((s32[]{:T(128)}, f32[1,128,8,80]{1,3,2,0:T(8,128)}, ...), condition=%wide.region_7.8_spmd.clone, body=%wide.region_6.7_spmd.clone.sunk | while | flops 1094352896 | bytes 14656932 | solution.py:144
  421.7 4.8 fusion.99
  426.5 2.0 constant_dynamic-slice_fusion.18
  429.4 2.9 multiply_convert_fusion.6
  435.2 4.8 fusion.99
  440.0 2.0 constant_dynamic-slice_fusion.18
  442.8 2.9 multiply_convert_fusion.6
  445.7 2.5 fusion.100
  449.6 4.8 fusion.99
  454.4 2.0 constant_dynamic-slice_fusion.18
  457.3 2.9 multiply_convert_fusion.6
  460.2 2.5 fusion.100
  464.1 4.8 fusion.99
  468.9 2.0 constant_dynamic-slice_fusion.18
  471.7 2.9 multiply_convert_fusion.6
  474.6 2.5 fusion.100
  477.0 1.7 multiply_convert_fusion.3
  478.7 76.3 %while.56 = (s32[]{:T(128)}, f32[1,128,8,80]{1,3,2,0:T(8,128)S(1)}, f32[1,128,8,80]{1,3,2,0:T(8,128)}, f32[1,2048,640]{2,1,0:T(8,128)}, pred[1,16,1]{1,2,0:T(4,1...) while((s32[]{:T(128)}, f32[1,128,8,80]{1,3,2,0:T(8,128)S(1)}, ...), condition=%wide.region_9.10_spmd.clone, body=%wide.region_8.9_spmd.clone.sunk | while | flops 1178927104 | bytes 26019420 | solution.py:222
  482.6 5.4 exponential_select_fusion.2
  488.0 2.0 constant_dynamic-slice_fusion.20
  491.3 2.9 multiply_convert_fusion.7
  494.2 2.5 fusion.109
  501.6 5.4 exponential_select_fusion.2
  507.0 2.0 constant_dynamic-slice_fusion.20
  510.4 2.9 multiply_convert_fusion.7
  513.3 2.5 fusion.109
  520.7 5.4 exponential_select_fusion.2
  526.1 2.0 constant_dynamic-slice_fusion.20
  529.4 2.9 multiply_convert_fusion.7
  532.3 2.5 fusion.109
  539.8 5.4 exponential_select_fusion.2
  545.2 2.0 constant_dynamic-slice_fusion.20
  548.5 2.9 multiply_convert_fusion.7
  551.4 2.5 fusion.109
  556.2 2.0 fusion.21
  560.5 3.2 collective-permute-start
  563.7 9.3 %collective-permute-done = bf16[1,1,128,1280]{3,2,1,0:T(8,128)(2,1)S(1)} collective-permute-done((bf16[1,1,128,1280]{3,2,1,0:T(8,128)(2,1)S(1)}, bf16[1,1,128,1280]{3,2,1,0:T(8,128)(2,1)S(1)}, u32[]{:S(2)}, u32[]{:S(2)}) %collective-permute-start) | collective-permute-done | bytes 327712 | tf_op jit(solution)/shard_map/ppermute | solution.py:15
  (165 shorter events, 61.4 us)
Async XLA Ops:
  6.5 111.3 %copy-start = (bf16[1,1,128,1280]{3,2,1,0:T(8,128)(2,1)S(1)}, bf16[1,1,128,1280]{3,2,1,0:T(8,128)(2,1)}, u32[]{:S(2)}) copy-start(bf16[1,1,128,1280]{3,2,1,0:T(8,128)(2,1)} %param.14) | copy-start | bytes 983044
  6.5 39.0 %copy-start.2 = (bf16[1,1,128,1280]{3,2,1,0:T(8,128)(2,1)S(1)}, bf16[1,1,128,1280]{3,2,1,0:T(8,128)(2,1)}, u32[]{:S(2)}) copy-start(bf16[1,1,128,1280]{3,2,1,0:T(8,128)(2,1)} %param.13) | copy-start | bytes 983044
  6.5 39.0 %all-gather.17.cloned.1.call-start = ((), (), s32[]{:S(2)}) async-start(), calls=%async_computation.2 | async-start | bytes 2048000 | tf_op jit(solution)/shard_map/all_gather | solution.py:232
  7.3 74.4 %all-gather.13.cloned.1.call-start = ((), (), s32[]{:S(2)}) async-start(), calls=%async_computation | async-start | bytes 2048000 | tf_op jit(solution)/shard_map/all_gather | solution.py:231
  8.0 109.8 %all-gather.19.cloned.1.call-start = ((), (), s32[]{:S(2)}) async-start(), calls=%async_computation.3 | async-start | bytes 2048000 | tf_op jit(solution)/shard_map/all_gather | solution.py:233
  8.7 145.1 %all-gather.15.cloned.1.call-start = ((), (), s32[]{:S(2)}) async-start(), calls=%async_computation.1 | async-start | bytes 2048000 | tf_op jit(solution)/shard_map/all_gather | solution.py:230
  9.3 223.0 %all-gather.23.cloned.1.call-start = ((), (), s32[]{:S(2)}) async-start(), calls=%async_computation.5 | async-start | bytes 2785280 | tf_op jit(solution)/shard_map/all_gather | solution.py:257
  48.3 263.2 %all-gather.21.cloned.1.call-start = ((), (), s32[]{:S(2)}) async-start(), calls=%async_computation.4 | async-start | bytes 5570560 | tf_op jit(solution)/shard_map/all_gather | solution.py:256
  84.5 39.3 %copy-start.9 = (f32[128,640]{1,0:T(8,128)S(1)}, f32[128,640]{1,0:T(8,128)}, u32[]{:S(2)}) copy-start(f32[128,640]{1,0:T(8,128)} %fusion.26) | copy-start | bytes 983044
  84.5 40.2 %copy-start.10 = (bf16[128,640]{1,0:T(8,128)(2,1)S(1)}, bf16[128,640]{1,0:T(8,128)(2,1)}, u32[]{:S(2)}) copy-start(bf16[128,640]{1,0:T(8,128)(2,1)} %fusion.28) | copy-start | bytes 491524
  84.5 394.2 %all-gather.27.cloned.1.call-start = ((), (), s32[]{:S(2)}) async-start(), calls=%async_computation.7 | async-start | bytes 2785280 | tf_op jit(solution)/shard_map/all_gather | solution.py:284
  120.6 358.1 %all-gather.25.cloned.1.call-start = ((), (), s32[]{:S(2)}) async-start(), calls=%async_computation.6 | async-start | bytes 5570560 | tf_op jit(solution)/shard_map/all_gather | solution.py:283
  155.9 1.3 copy-start.8
  420.3 58.4 %copy-start.1 = (f32[1,128,8,80]{1,3,2,0:T(8,128)S(1)}, f32[1,128,8,80]{1,3,2,0:T(8,128)}, u32[]{:S(2)}) copy-start(f32[1,128,8,80]{1,3,2,0:T(8,128)} %custom-call.4) | copy-start | bytes 983044
  478.7 3.7 copy-start.12
  478.7 3.8 copy-start.11
  494.2 2.5 copy-start.4
  497.1 0.7 copy-start.5
  497.8 3.7 copy-start.12
  497.8 3.8 copy-start.11
  513.3 2.5 copy-start.4
  516.2 0.7 copy-start.5
  516.9 3.7 copy-start.12
  516.9 3.8 copy-start.11
  532.3 2.5 copy-start.4
  535.2 0.7 copy-start.5
  536.0 3.7 copy-start.12
  536.0 3.8 copy-start.11
  551.4 2.5 copy-start.4
  554.3 0.7 copy-start.5
  555.0 3.2 copy-start.7
  558.2 1.0 copy-start.3
  558.2 1.5 copy-start.6
  560.5 12.6 %collective-permute-start = (bf16[1,1,128,1280]{3,2,1,0:T(8,128)(2,1)S(1)}, bf16[1,1,128,1280]{3,2,1,0:T(8,128)(2,1)S(1)}, u32[]{:S(2)}, u32[]{:S(2)}) collective-permute-start(bf16[1,1,128,1280]{3,2,1,0:T(8,128)(2,1)S(1)} %fusion.44), channel_id=1, source_target_pairs={{0,448},{64,0},{128,64},{192,128},{256,192},{320,256},{384,320},{4... | collective-permute-start | bytes 983048 | tf_op jit(solution)/shard_map/ppermute | solution.py:15
Sparse Core Ops, SparseCore 0:
  9.5 36.0 all-gather.16
  47.7 33.9 all-gather.12
  83.8 33.9 all-gather.18
  119.8 33.9 all-gather.14
  155.7 76.5 all-gather.22
  234.3 77.2 all-gather.20
  313.6 71.2 all-gather.26
  387.0 77.6 all-gather.24
where the time goes:
time: 583 us; the launch traced here: 581 us
  waiting for transfers between devices  292 us (50%)
  matrix products  120 us (21%)
  local copies, waits for them, and re-layouts  83.9 us (14%)
  blocking collectives  60.5 us (10%)
  between operations  13.7 us (2%)
  other arithmetic  6.74 us (1%)
    all_gather x1, waiting for transfers between devices, body(): lax.all_gather(key_rows, 'ctx', axis=1, tiled=True)  74.7 us
    all_gather x1, waiting for transfers between devices, body(): lax.all_gather(value_rows.astype(jnp.float32), 'ctx', axis=1, tiled=True)  74.2 us
    all_gather x1, waiting for transfers between devices, body(): lax.all_gather(value_weight, 'dp', axis=2, tiled=True)  35.1 us
    all_gather x1, waiting for transfers between devices, body(): lax.all_gather(key_weight, 'dp', axis=2, tiled=True)  33.3 us
    all_gather x1, waiting for transfers between devices, body(): lax.all_gather(out_weight, 'dp', axis=1, tiled=True)  33.3 us
    all_gather x1, blocking collectives, body(): lax.all_gather(row_delta, 'ctx', axis=1, tiled=True)  30.9 us
    all_gather x1, blocking collectives, body(): lax.all_gather(log_total, 'ctx', axis=1, tiled=True)  29.6 us
    all_gather x1, waiting for transfers between devices, body(): lax.all_gather(query_weight, 'dp', axis=2, tiled=True)  28.9 us
  transfers between devices with their start and end apart: 9, of which 7 were waited for; matrix products, arithmetic and copies ran while one was open for 22% of the time, Pallas kernels for 0%

commit v1 on v0

--- a/solution.py
+++ b/solution.py
@@ -262,7 +262,9 @@
     )
     all_log_total, all_delta = (
         lax.all_gather(log_total, "ctx", axis=1, tiled=True),
-        lax.all_gather(row_delta, "ctx", axis=1, tiled=True),
+        jnp.concatenate(
+            lax.all_to_all(jnp.stack([row_delta] * lax.axis_size("ctx")), "ctx", 0, 0), axis=1
+        ),
     )
     q_grad = query_side(
         queries,

time: 583 us -> 569 us (0.976)
  the two profiles are of different devices: /device:TPU:62 before, /device:TPU:28 now
where the time goes in v1:
time: 569 us; the launch traced here: 566 us
  waiting for transfers between devices  309 us (54%)
  matrix products  124 us (22%)
  local copies, waits for them, and re-layouts  72.5 us (13%)
  blocking collectives  30.2 us (5%)
  between operations  13.7 us (2%)
  starting transfers between devices  9.5 us (2%)
  other arithmetic  6.72 us (1%)
    all_gather x1, waiting for transfers between devices, body(): lax.all_gather(value_rows.astype(jnp.float32), 'ctx', axis=1, tiled=True)  75.4 us
    all_gather x1, waiting for transfers between devices, body(): lax.all_gather(key_rows, 'ctx', axis=1, tiled=True)  74.9 us
    all_gather x1, waiting for transfers between devices, body(): lax.all_gather(value_weight, 'dp', axis=2, tiled=True)  35.2 us
    all_gather x1, waiting for transfers between devices, body(): lax.all_gather(key_weight, 'dp', axis=2, tiled=True)  33.3 us
    all_gather x1, waiting for transfers between devices, body(): lax.all_gather(out_weight, 'dp', axis=1, tiled=True)  33.2 us
    all_gather x1, blocking collectives, body(): lax.all_gather(log_total, 'ctx', axis=1, tiled=True)  30.2 us
    all_gather x1, waiting for transfers between devices, body(): lax.all_gather(query_weight, 'dp', axis=2, tiled=True)  28.2 us
    dot_general x4, matrix products, key_visit(): jnp.einsum('bphd,brhd->bhpr', query_part, key_four, precision=HIGHEST, pr...  21.8 us
  transfers between devices with their start and end apart: 10, of which 8 were waited for; matrix products, arithmetic and copies ran while one was open for 21% of the time, Pallas kernels for 0%

profile of v1, /device:TPU:28, one launch (start us, length us, event | category | flops | bytes accessed | tf_op | source)
XLA Modules:
  0.0 566.5 jit_solution(12936515090894765828)
XLA Ops:
  11.1 35.2 %all-gather.17.cloned.1.call-done = bf16[1,1280,640]{1,2,0:T(8,128)(2,1)} async-done(((bf16[1,1280,160]{1,2,0:T(8,128)(2,1)}), bf16[1,1280,640]{1,2,0:T(8,128)(2,1)}) %all-gather.17.cloned.1.call-update) | async-done | bytes 1638416 | tf_op jit(solution)/shard_map/all_gather | solution.py:232
  46.3 2.7 fusion.28
  49.1 33.3 %all-gather.13.cloned.1.call-done = bf16[1,1280,640]{1,2,0:T(8,128)(2,1)} async-done(((bf16[1,1280,160]{1,2,0:T(8,128)(2,1)}), bf16[1,1280,640]{1,2,0:T(8,128)(2,1)}) %all-gather.13.cloned.1.call-update) | async-done | bytes 1638416 | tf_op jit(solution)/shard_map/all_gather | solution.py:231
  82.4 2.8 fusion.26
  85.3 33.2 %all-gather.19.cloned.1.call-done = bf16[1,640,1280]{2,1,0:T(8,128)(2,1)} async-done(((bf16[1,160,1280]{2,1,0:T(8,128)(2,1)}), bf16[1,640,1280]{2,1,0:T(8,128)(2,1)}) %all-gather.19.cloned.1.call-update) | async-done | bytes 1638416 | tf_op jit(solution)/shard_map/all_gather | solution.py:233
  118.5 2.7 fusion.31
  122.9 1.7 copy.34
  126.3 28.2 %all-gather.15.cloned.1.call-done = bf16[1,1280,640]{1,2,0:T(8,128)(2,1)} async-done(((bf16[1,1280,160]{1,2,0:T(8,128)(2,1)}), bf16[1,1280,640]{1,2,0:T(8,128)(2,1)}) %all-gather.15.cloned.1.call-update) | async-done | bytes 1638416 | tf_op jit(solution)/shard_map/all_gather | solution.py:230
  154.5 2.1 fusion.23
  157.4 75.4 %all-gather.23.cloned.1.call-done = bf16[2048,640]{1,0:T(8,128)(2,1)} async-done(((bf16[128,640]{1,0:T(8,128)(2,1)}), bf16[2048,640]{1,0:T(8,128)(2,1)}) %all-gather.23.cloned.1.call-update) | async-done | bytes 2621456 | tf_op jit(solution)/shard_map/all_gather | solution.py:257
  232.8 4.5 copy.37
  237.2 74.9 %all-gather.21.cloned.1.call-done = f32[2048,640]{1,0:T(8,128)} async-done(((f32[128,640]{1,0:T(8,128)}), f32[2048,640]{1,0:T(8,128)}) %all-gather.21.cloned.1.call-update) | async-done | bytes 5242896 | tf_op jit(solution)/shard_map/all_gather | solution.py:256
  312.2 6.0 %copy.38 = f32[1,2048,640]{1,2,0:T(8,128)} copy(f32[1,2048,640]{2,1,0:T(8,128)} %bitcast.279) | data formatting | bytes 10485760
  318.2 35.6 %while.54 = (s32[]{:T(128)}, f32[1,8,128]{2,1,0:T(8,128)S(1)}, f32[1,8,128]{2,1,0:T(8,128)S(1)}, f32[1,8,128]{2,1,0:T(8,128)S(1)}, pred[1,1,16]{2,1,0:T(4,128)(4...) while((s32[]{:T(128)}, f32[1,8,128]{2,1,0:T(8,128)S(1)}, ...), condition=%wide.region_5.6_spmd.clone, body=%wide.region_1.5_spmd.clone.sunk | while | flops 594549760 | bytes 12757413 | solution.py:78
  320.9 3.6 bitcast_reduce_fusion.2
  324.5 1.9 fusion.91
  329.8 3.6 bitcast_reduce_fusion.2
  333.4 1.9 fusion.91
  338.7 3.6 bitcast_reduce_fusion.2
  342.3 1.9 fusion.91
  347.6 3.6 bitcast_reduce_fusion.2
  351.2 1.9 fusion.91
  354.4 6.8 %all-to-all-start = ((f32[16,1,128,8]{2,3,1,0:T(8,128)}), f32[16,1,128,8]{2,3,1,0:T(8,128)S(1)}, u32[]{:S(2)}, u32[]{:S(2)}) async-start(f32[16,1,128,8]{2,3,1,0:T(8,128)} %stack.2), calls=%async_computation | async-start | bytes 131072 | tf_op jit(solution)/shard_map/all_to_all | solution.py:266
  361.2 30.2 %all_gather.34 = f32[1,2048,8]{1,2,0:T(8,128)S(1)} all-gather(f32[1,128,8]{1,2,0:T(8,128)S(1)} %bitcast.291), channel_id=1, replica_groups=mesh['section'=8,'ctx'=16,'dp'=4] {'ctx'}, dimensions={1}, use_global_device_ids=true | all-gather | bytes 69632 | tf_op jit(solution)/shard_map/all_gather | solution.py:264
  391.4 55.9 %while.55 = (s32[]{:T(128)}, f32[1,128,8,80]{1,3,2,0:T(8,128)}, f32[1,2048,640]{1,2,0:T(8,128)}, pred[1,1,16]{2,1,0:T(4,128)(4,1)}, f32[1,128,8,80]{1,3,2,0:T(8,...) while((s32[]{:T(128)}, f32[1,128,8,80]{1,3,2,0:T(8,128)}, ...), condition=%wide.region_7.8_spmd.clone, body=%wide.region_6.7_spmd.clone.sunk | while | flops 1094352896 | bytes 17933908 | solution.py:144
  392.8 4.8 fusion.99
  399.0 3.6 multiply_convert_fusion.6
  402.5 2.1 fusion.100
  406.8 4.8 fusion.99
  412.9 3.6 multiply_convert_fusion.6
  416.5 2.1 fusion.100
  419.3 1.4 constant_dynamic-slice_fusion.17
  420.8 4.8 fusion.99
  426.9 3.6 multiply_convert_fusion.6
  430.5 2.1 fusion.100
  434.8 4.8 fusion.99
  440.9 3.6 multiply_convert_fusion.6
  444.5 2.1 fusion.100
  448.4 2.8 fusion.21
  451.1 15.7 %all-gather.25.cloned.1.call-done = f32[2048,640]{1,0:T(8,128)} async-done(((f32[128,640]{1,0:T(8,128)}), f32[2048,640]{1,0:T(8,128)}) %all-gather.25.cloned.1.call-update) | async-done | bytes 5242896 | tf_op jit(solution)/shard_map/all_gather | solution.py:285
  466.9 75.3 %while.56 = (s32[]{:T(128)}, f32[1,128,8,80]{1,3,2,0:T(8,128)S(1)}, f32[1,128,8,80]{1,3,2,0:T(8,128)}, f32[1,2048,640]{2,1,0:T(8,128)}, pred[1,16,1]{1,2,0:T(4,1...) while((s32[]{:T(128)}, f32[1,128,8,80]{1,3,2,0:T(8,128)S(1)}, ...), condition=%wide.region_9.10_spmd.clone, body=%wide.region_8.9_spmd.clone.sunk | while | flops 1178927104 | bytes 24708584 | solution.py:222
  468.3 1.5 copy.49
  470.5 5.4 exponential_select_fusion.2
  475.9 2.0 constant_dynamic-slice_fusion.20
  479.3 2.8 multiply_convert_fusion.7
  482.1 2.5 fusion.109
  487.1 1.5 copy.49
  489.3 5.4 exponential_select_fusion.2
  494.8 2.0 constant_dynamic-slice_fusion.20
  498.1 2.8 multiply_convert_fusion.7
  500.9 2.5 fusion.109
  505.9 1.5 copy.49
  508.1 5.4 exponential_select_fusion.2
  513.6 2.0 constant_dynamic-slice_fusion.20
  516.9 2.8 multiply_convert_fusion.7
  519.7 2.5 fusion.109
  524.8 1.5 copy.49
  527.0 5.4 exponential_select_fusion.2
  532.4 2.0 constant_dynamic-slice_fusion.20
  535.8 2.8 multiply_convert_fusion.7
  538.6 2.5 fusion.109
  543.4 2.0 convolution_add_fusion.1
  546.3 2.4 collective-permute-start
  548.8 10.2 %collective-permute-done = bf16[1,1,128,1280]{3,2,1,0:T(8,128)(2,1)S(1)} collective-permute-done((bf16[1,1,128,1280]{3,2,1,0:T(8,128)(2,1)S(1)}, bf16[1,1,128,1280]{3,2,1,0:T(8,128)(2,1)S(1)}, u32[]{:S(2)}, u32[]{:S(2)}) %collective-permute-start) | collective-permute-done | bytes 327712 | tf_op jit(solution)/shard_map/ppermute | solution.py:15
  (186 shorter events, 56.7 us)
Async XLA Ops:
  6.5 112.0 %copy-start = (bf16[1,1,128,1280]{3,2,1,0:T(8,128)(2,1)S(1)}, bf16[1,1,128,1280]{3,2,1,0:T(8,128)(2,1)}, u32[]{:S(2)}) copy-start(bf16[1,1,128,1280]{3,2,1,0:T(8,128)(2,1)} %param.14) | copy-start | bytes 983044
  6.5 39.8 %copy-start.4 = (bf16[1,1,128,1280]{3,2,1,0:T(8,128)(2,1)S(1)}, bf16[1,1,128,1280]{3,2,1,0:T(8,128)(2,1)}, u32[]{:S(2)}) copy-start(bf16[1,1,128,1280]{3,2,1,0:T(8,128)(2,1)} %param.13) | copy-start | bytes 983044
  6.5 39.7 %all-gather.17.cloned.1.call-start = ((), (), s32[]{:S(2)}) async-start(), calls=%async_computation.3 | async-start | bytes 2048000 | tf_op jit(solution)/shard_map/all_gather | solution.py:232
  7.3 75.1 %all-gather.13.cloned.1.call-start = ((), (), s32[]{:S(2)}) async-start(), calls=%async_computation.1 | async-start | bytes 2048000 | tf_op jit(solution)/shard_map/all_gather | solution.py:231
  8.0 110.5 %all-gather.19.cloned.1.call-start = ((), (), s32[]{:S(2)}) async-start(), calls=%async_computation.4 | async-start | bytes 2048000 | tf_op jit(solution)/shard_map/all_gather | solution.py:233
  8.7 145.8 %all-gather.15.cloned.1.call-start = ((), (), s32[]{:S(2)}) async-start(), calls=%async_computation.2 | async-start | bytes 2048000 | tf_op jit(solution)/shard_map/all_gather | solution.py:230
  9.3 223.5 %all-gather.23.cloned.1.call-start = ((), (), s32[]{:S(2)}) async-start(), calls=%async_computation.6 | async-start | bytes 2785280 | tf_op jit(solution)/shard_map/all_gather | solution.py:257
  11.1 143.4 %copy-start.13 = (f32[128]{0:T(128)}, f32[128]{0:T(128)S(1)}, u32[]{:S(2)}) copy-start(f32[128]{0:T(128)S(1)} %get-tuple-element.941) | copy-start | bytes 1540
  49.1 263.1 %all-gather.21.cloned.1.call-start = ((), (), s32[]{:S(2)}) async-start(), calls=%async_computation.5 | async-start | bytes 5570560 | tf_op jit(solution)/shard_map/all_gather | solution.py:256
  85.2 39.4 %copy-start.10 = (f32[128,640]{1,0:T(8,128)S(1)}, f32[128,640]{1,0:T(8,128)}, u32[]{:S(2)}) copy-start(f32[128,640]{1,0:T(8,128)} %fusion.26) | copy-start | bytes 983044
  85.2 40.2 %copy-start.11 = (bf16[128,640]{1,0:T(8,128)(2,1)S(1)}, bf16[128,640]{1,0:T(8,128)(2,1)}, u32[]{:S(2)}) copy-start(bf16[128,640]{1,0:T(8,128)(2,1)} %fusion.28) | copy-start | bytes 491524
  85.2 365.9 %all-gather.27.cloned.1.call-start = ((), (), s32[]{:S(2)}) async-start(), calls=%async_computation.8 | async-start | bytes 2785280 | tf_op jit(solution)/shard_map/all_gather | solution.py:286
  121.3 345.6 %all-gather.25.cloned.1.call-start = ((), (), s32[]{:S(2)}) async-start(), calls=%async_computation.7 | async-start | bytes 5570560 | tf_op jit(solution)/shard_map/all_gather | solution.py:285
  156.6 0.7 copy-start.9
  353.7 0.6 copy-start.16
  354.4 112.5 %all-to-all-start = ((f32[16,1,128,8]{2,3,1,0:T(8,128)}), f32[16,1,128,8]{2,3,1,0:T(8,128)S(1)}, u32[]{:S(2)}, u32[]{:S(2)}) async-start(f32[16,1,128,8]{2,3,1,0:T(8,128)} %stack.2), calls=%async_computation | async-start | bytes 131072 | tf_op jit(solution)/shard_map/all_to_all | solution.py:266
  392.8 6.0 %copy-start.17 = (pred[1,1,16]{2,1,0:T(4,128)(4,1)S(1)}, pred[1,1,16]{2,1,0:T(4,128)(4,1)}, u32[]{:S(2)}) copy-start(pred[1,1,16]{2,1,0:T(4,128)(4,1)} %get-tuple-element.1215) | copy-start | bytes 52 | tf_op jit(solution)/shard_map/while
  392.8 6.1 %copy-start.12 = (bf16[1,128,8,80]{1,3,2,0:T(8,128)(2,1)S(1)}, bf16[1,128,8,80]{1,3,2,0:T(8,128)(2,1)}, u32[]{:S(2)}) copy-start(bf16[1,128,8,80]{1,3,2,0:T(8,128)(2,1)} %get-tuple-element.1219) | copy-start | bytes 491524 | tf_op jit(solution)/shard_map/while
  399.0 3.6 copy-start.2
  404.6 0.7 copy-start.3
  406.8 6.0 %copy-start.17 = (pred[1,1,16]{2,1,0:T(4,128)(4,1)S(1)}, pred[1,1,16]{2,1,0:T(4,128)(4,1)}, u32[]{:S(2)}) copy-start(pred[1,1,16]{2,1,0:T(4,128)(4,1)} %get-tuple-element.1215) | copy-start | bytes 52 | tf_op jit(solution)/shard_map/while
  406.8 6.1 %copy-start.12 = (bf16[1,128,8,80]{1,3,2,0:T(8,128)(2,1)S(1)}, bf16[1,128,8,80]{1,3,2,0:T(8,128)(2,1)}, u32[]{:S(2)}) copy-start(bf16[1,128,8,80]{1,3,2,0:T(8,128)(2,1)} %get-tuple-element.1219) | copy-start | bytes 491524 | tf_op jit(solution)/shard_map/while
  412.9 3.6 copy-start.2
  418.6 0.7 copy-start.3
  420.7 6.0 %copy-start.17 = (pred[1,1,16]{2,1,0:T(4,128)(4,1)S(1)}, pred[1,1,16]{2,1,0:T(4,128)(4,1)}, u32[]{:S(2)}) copy-start(pred[1,1,16]{2,1,0:T(4,128)(4,1)} %get-tuple-element.1215) | copy-start | bytes 52 | tf_op jit(solution)/shard_map/while
  420.8 6.2 %copy-start.12 = (bf16[1,128,8,80]{1,3,2,0:T(8,128)(2,1)S(1)}, bf16[1,128,8,80]{1,3,2,0:T(8,128)(2,1)}, u32[]{:S(2)}) copy-start(bf16[1,128,8,80]{1,3,2,0:T(8,128)(2,1)} %get-tuple-element.1219) | copy-start | bytes 491524 | tf_op jit(solution)/shard_map/while
  426.9 3.6 copy-start.2
  432.6 0.7 copy-start.3
  434.7 6.0 %copy-start.17 = (pred[1,1,16]{2,1,0:T(4,128)(4,1)S(1)}, pred[1,1,16]{2,1,0:T(4,128)(4,1)}, u32[]{:S(2)}) copy-start(pred[1,1,16]{2,1,0:T(4,128)(4,1)} %get-tuple-element.1215) | copy-start | bytes 52 | tf_op jit(solution)/shard_map/while
  434.7 6.1 %copy-start.12 = (bf16[1,128,8,80]{1,3,2,0:T(8,128)(2,1)S(1)}, bf16[1,128,8,80]{1,3,2,0:T(8,128)(2,1)}, u32[]{:S(2)}) copy-start(bf16[1,128,8,80]{1,3,2,0:T(8,128)(2,1)} %get-tuple-element.1219) | copy-start | bytes 491524 | tf_op jit(solution)/shard_map/while
  440.9 3.6 copy-start.2
  446.6 0.7 copy-start.3
  447.3 19.6 %copy-start.1 = (f32[1,128,8,80]{1,3,2,0:T(8,128)S(1)}, f32[1,128,8,80]{1,3,2,0:T(8,128)}, u32[]{:S(2)}) copy-start(f32[1,128,8,80]{1,3,2,0:T(8,128)} %custom-call.4) | copy-start | bytes 983044
  482.1 2.5 copy-start.6
  485.0 0.7 copy-start.7
  500.9 2.5 copy-start.6
  503.8 0.7 copy-start.7
  519.7 2.5 copy-start.6
  522.6 0.7 copy-start.7
  538.6 2.5 copy-start.6
  541.5 0.7 copy-start.7
  542.2 3.2 copy-start.5
  542.2 3.2 copy-start.8
  545.4 0.6 copy-start.14
  545.4 0.7 copy-start.15
  546.3 12.6 %collective-permute-start = (bf16[1,1,128,1280]{3,2,1,0:T(8,128)(2,1)S(1)}, bf16[1,1,128,1280]{3,2,1,0:T(8,128)(2,1)S(1)}, u32[]{:S(2)}, u32[]{:S(2)}) collective-permute-start(bf16[1,1,128,1280]{3,2,1,0:T(8,128)(2,1)S(1)} %fusion.44), channel_id=1, source_target_pairs={{0,448},{64,0},{128,64},{192,128},{256,192},{320,256},{384,320},{4... | collective-permute-start | bytes 983048 | tf_op jit(solution)/shard_map/ppermute | solution.py:15
Sparse Core Ops, SparseCore 0:
  9.5 36.7 all-gather.16
  48.4 33.9 all-gather.12
  84.5 33.9 all-gather.18
  120.5 33.9 all-gather.14
  156.4 76.3 all-gather.22
  234.7 77.3 all-gather.20
  314.2 72.2 all-gather.26
  388.6 78.1 all-gather.24
